TPU v7x, 32 devices: a whole 2x2x4 slice. The times are simulated.
32 devices in a mesh: alpha: 8 (over z, x), beta: 4 (over y, core).
Axes of the slice: x: 2, y: 2, z: 4, core: 2. Of those that a mesh axis runs over, the one named last changes fastest.
Arguments:
- coeffs: bfloat16 [2048, 4096], P('alpha', 'beta'), may hold values from -6 to 6
- a_blocks: bfloat16 [2, 2048, 11, 128], P(None, 'alpha'), may hold values from -0.15625 to 0.15625
- a_list: int32 [2, 16, 11], replicated, may hold values from 0 to 15, as said below
- a_count: int32 [2, 16], replicated, may hold values from 4 to 11, as said below
- b_blocks: bfloat16 [2, 4096, 11, 128], P(None, 'beta'), may hold values from -0.15625 to 0.15625
- b_list: int32 [2, 32, 11], replicated, may hold values from 0 to 31, as said below
- b_count: int32 [2, 32], replicated, may hold values from 4 to 11, as said below
Outputs:
- sigma: float32 [2048, 4096], P('alpha', 'beta')
Inputs may be any that keep to these rules, and one draw needn't show every extreme that they name: `a_list`: every entry, valid slot or not, is an alpha block number. For each index r of alpha and each index o of alpha, the entries of all operators in the rows of blocks r * 2 to r * 2 + 1 that lie in blocks o * 2 to o * 2 + 1 name at most 1 distinct blocks, and some pair names exactly 1. `b_list`: the same with beta, 8 and 2. `a_count`: some row has all 11 slots valid. `b_count`: some row has all 11 slots valid.
All inputs are finite; a program needn't handle non-finite values.
Results may differ from a plain program's by a relative error of at most 0.0029.
Values may be sent and summed in bfloat16 or wider, within the bound.
A program may use at most 128 MiB of HBM per device.

v0:
```python
import jax
import jax.numpy as jnp
from jax import lax
from jax.sharding import PartitionSpec as P

FROM_A = 1
FROM_B = 2


def arrange(entries, owners, per_owner, capacity):
    operators, total, list_slots = entries.shape
    flattened = entries.reshape(operators, owners, per_owner * list_slots)
    matches = flattened[..., None] == jnp.arange(total, dtype=jnp.int32)
    present = jnp.any(matches, axis=(0, 2)).reshape(owners, owners, per_owner).astype(jnp.int32)
    ranking = jnp.cumsum(present, axis=2)
    position = jnp.arange(capacity, dtype=jnp.int32) + 1
    chosen_bits = (present[..., None] == 1) & (ranking[..., None] == position)
    local_ids = jnp.arange(per_owner, dtype=jnp.int32)[None, None, :, None]
    wanted = jnp.sum(local_ids * chosen_bits.astype(jnp.int32), axis=2)
    return (wanted, ranking)


def locate(entries, ranking_here, per_owner, capacity):
    owner = entries // per_owner
    local_id = entries % per_owner
    return owner * capacity + ranking_here[owner, local_id] - 1


def pick_columns(pool_piece, index_piece):
    return pool_piece[:, index_piece]


def on_device(coeffs, a_blocks, a_list, a_count, b_blocks, b_list, b_count):
    operators, local_rows, list_slots, block_size = a_blocks.shape
    local_cols = coeffs.shape[1]
    row_blocks = local_rows // block_size
    col_blocks = local_cols // block_size
    row_capacity = FROM_A
    col_capacity = FROM_B
    alpha_size = lax.axis_size("alpha")
    beta_size = lax.axis_size("beta")
    alpha_here = lax.axis_index("alpha")
    beta_here = lax.axis_index("beta")
    slot_ids = jnp.arange(list_slots, dtype=jnp.int32)
    alpha_mine = lax.dynamic_slice_in_dim(a_list, alpha_here * row_blocks, row_blocks, 1)
    alpha_counts = lax.dynamic_slice_in_dim(a_count, alpha_here * row_blocks, row_blocks, 1)
    alpha_valid = slot_ids < alpha_counts[..., None]
    alpha_kept = jnp.where(
        alpha_valid[:, :, None, :, None],
        a_blocks.reshape(operators, row_blocks, block_size, list_slots, block_size),
        jnp.zeros((), jnp.bfloat16),
    )
    wanted, ranking = arrange(a_list, alpha_size, row_blocks, row_capacity)
    outgoing = coeffs.reshape(row_blocks, block_size, local_cols)[wanted[:, alpha_here, :]]
    incoming = lax.all_to_all(outgoing, "alpha", split_axis=0, concat_axis=0, tiled=True)
    source_index = locate(alpha_mine, ranking[alpha_here], row_blocks, row_capacity)
    chosen = incoming.reshape(alpha_size * row_capacity, block_size, local_cols)[source_index]
    inter = jnp.einsum("kbrsi,kbsic->kbrc", alpha_kept, chosen, preferred_element_type=jnp.float32)
    inter = inter.astype(jnp.bfloat16).reshape(operators, local_rows, col_blocks, block_size)
    wanted_cols, ranking_cols = arrange(b_list, beta_size, col_blocks, col_capacity)
    outgoing_cols = inter[:, :, wanted_cols[:, beta_here, :], :]
    incoming_cols = lax.all_to_all(outgoing_cols, "beta", split_axis=2, concat_axis=2, tiled=True)
    beta_mine = lax.dynamic_slice_in_dim(b_list, beta_here * col_blocks, col_blocks, 1)
    beta_counts = lax.dynamic_slice_in_dim(b_count, beta_here * col_blocks, col_blocks, 1)
    beta_valid = slot_ids < beta_counts[..., None]
    beta_kept = jnp.where(
        beta_valid[:, :, None, :, None],
        b_blocks.reshape(operators, col_blocks, block_size, list_slots, block_size),
        jnp.zeros((), jnp.bfloat16),
    )
    source_cols = locate(beta_mine, ranking_cols[beta_here], col_blocks, col_capacity)
    pooled = incoming_cols.reshape(operators, local_rows, beta_size * col_capacity, block_size)
    picked = jax.vmap(pick_columns)(pooled, source_cols)
    sigma = jnp.einsum("kabsj,kbrsj->abr", picked, beta_kept, preferred_element_type=jnp.float32)
    return sigma.reshape(local_rows, local_cols)


def solution(mesh):
    in_specs = (
        P("alpha", "beta"),
        P(None, "alpha", None, None),
        P(),
        P(),
        P(None, "beta", None, None),
        P(),
        P(),
    )
    out_specs = P("alpha", "beta")
    return jax.shard_map(
        on_device, mesh=mesh, in_specs=in_specs, out_specs=out_specs, check_vma=False
    )
```

profile of v0, /device:TPU:0, one launch (start us, length us, event | category | flops | bytes accessed | tf_op | source)
XLA Modules:
  0.0 113.2 jit_solution(14768770134497655556)
XLA Ops:
  0.0 0.8 copy.47
  0.9 0.2 fusion.5
  1.3 0.1 copy.48
  1.5 2.0 %gather_fusion = bf16[8,128,1024]{2,1,0:T(8,128)(2,1)} fusion(bf16[2,128,1024]{2,1,0:T(8,128)(2,1)S(1)} %bitcast.62, s32[1024]{0:T(1024)S(1)} %pad_clamp_fusion.2), kind=kCustom, calls=%fused_computation | custom fusion | bytes 4194336 | tf_op jit(solution)/shard_map/gather | solution.py:54
  3.5 7.3 %all-to-all-start = ((bf16[8,1,128,1024]{3,2,1,0:T(8,128)(2,1)}), bf16[8,1,128,1024]{3,2,1,0:T(8,128)(2,1)S(1)}, u32[]{:S(2)}, u32[]{:S(2)}) async-start(bf16[8,1,128,1024]{3,2,1,0:T(8,128)(2,1)} %bitcast.68), calls=%async_computation | async-start | bytes 4194304 | tf_op jit(solution)/shard_map/all_to_all | solution.py:55
  11.0 0.1 copy.53
  11.1 1.1 gather_fusion.1
  12.1 0.1 reshape.174
  12.2 0.1 reshape.179
  12.3 0.1 copy.54
  12.4 0.1 eq.94
  12.5 0.2 fusion.6
  12.7 0.7 reduce_window_sum.23
  13.5 0.3 select_reduce_fusion
  13.8 0.1 copy.55
  13.9 0.1 copy.56
  14.0 0.1 reshape.187
  14.3 44.7 %all-to-all-done = bf16[8,1,128,1024]{3,2,1,0:T(8,128)(2,1)S(1)} async-done(((bf16[8,1,128,1024]{3,2,1,0:T(8,128)(2,1)}), bf16[8,1,128,1024]{3,2,1,0:T(8,128)(2,1)S(1)}, u32[]{:S(2)}, u32[]{:S(2)}) %all-to-all-start) | async-done | bytes 2097184 | tf_op jit(solution)/shard_map/all_to_all | solution.py:55
  59.0 6.1 %gather_fusion.2 = bf16[44,128,1024]{2,1,0:T(8,128)(2,1)} fusion(bf16[8,128,1024]{2,1,0:T(8,128)(2,1)S(1)} %bitcast.65, s32[1024]{0:T(1024)S(1)} %pad_clamp_fusion.1), kind=kCustom, calls=%fused_computation.2 | custom fusion | bytes 23068848 | tf_op jit(solution)/shard_map/gather | solution.py:57
  65.1 6.6 %bitcast_convert_fusion = bf16[2,2,128,1024]{3,2,1,0:T(8,128)(2,1)S(1)} fusion(bf16[2,2,11,128,1024]{4,3,2,1,0:T(8,128)(2,1)} %bitcast.66, bf16[2,2,128,11,128]{4,2,1,3,0:T(8,128)(2,1)} %bitcast.71, pred[2,2,11]{2,1,0:T(4,128)(4,1)S(1)} %iota_compare_fusion.3), kind=kOutput, calls=%fused_computation.10 | convolution fusion | flops 1477640192 | bytes 14024748 | tf_op jit(solution)/shard_map/kbrsi,kbsic->kbrc/dot_general | solution.py:58
  71.7 0.3 copy.64
  72.0 0.2 copy.57
  72.2 1.7 %gather_fusion.3 = bf16[8,2,256,128]{3,2,1,0:T(8,128)(2,1)} fusion(bf16[2,256,8,128]{3,1,2,0:T(8,128)(2,1)S(1)} %copy.57, s32[1024]{0:T(1024)S(1)} %pad_clamp_fusion), kind=kCustom, calls=%fused_computation.3 | custom fusion | bytes 2097184 | tf_op jit(solution)/shard_map/gather | solution.py:61
  73.8 3.6 %all-to-all-start.1 = ((bf16[2,256,4,2,128]{4,1,0,3,2:T(8,128)(2,1)}), bf16[2,256,4,2,128]{4,1,0,3,2:T(8,128)(2,1)S(1)}, u32[]{:S(2)}, u32[]{:S(2)}) async-start(bf16[2,256,4,2,128]{4,1,0,3,2:T(8,128)(2,1)} %bitcast.15), calls=%async_computation.1 | async-start | bytes 2097152 | tf_op jit(solution)/shard_map/all_to_all | solution.py:62
  77.5 0.1 reshape.193
  77.6 2.7 %gather_fusion.4 = s32[176]{0:T(256)S(1)} fusion(s32[4,8]{1,0:T(4,128)S(1)} %dynamic-slice_bitcast_fusion, s32[176]{0:T(256)S(1)} %reshape.193), kind=kCustom, calls=%fused_computation.4 | custom fusion | bytes 2816 | tf_op jit(solution)/shard_map/gather | solution.py:26
  80.5 0.1 reshape.199
  80.7 11.2 %all-to-all-done.1 = bf16[2,256,4,2,128]{4,1,0,3,2:T(8,128)(2,1)S(1)} async-done(((bf16[2,256,4,2,128]{4,1,0,3,2:T(8,128)(2,1)}), bf16[2,256,4,2,128]{4,1,0,3,2:T(8,128)(2,1)S(1)}, u32[]{:S(2)}, u32[]{:S(2)}) %all-to-all-start.1) | async-done | bytes 1048608 | tf_op jit(solution)/shard_map/all_to_all | solution.py:62
  91.9 0.1 copy.58
  92.0 10.1 %gather_fusion.5 = bf16[176,256,128]{2,1,0:T(8,128)(2,1)} fusion(bf16[2,256,8,128]{3,1,2,0:T(8,128)(2,1)S(1)} %bitcast.64, s32[176]{0:T(256)S(1)} %reshape.199), kind=kCustom, calls=%fused_computation.5 | custom fusion | bytes 23070080 | tf_op jit(solution)/shard_map/vmap()/gather | solution.py:30
  102.1 9.8 %fusion = f32[8,128,256,1,1]{2,1,4,0,3:T(8,128)S(1)} fusion(bf16[2,256,8,11,128]{4,1,3,2,0:T(8,128)(2,1)} %bitcast.67, bf16[2,8,128,11,128]{4,2,1,3,0:T(8,128)(2,1)} %bitcast.74, pred[2,8,11]{2,1,0:T(8,128)(4,1)S(1)} %iota_compare_fusion.2), kind=kOutput, calls=%fused_computation.7 | convolution fusion | flops 1479278592 | bytes 18350256 | tf_op jit(solution)/shard_map/kabsj,kbrsj->abr/dot_general | solution.py:74
  111.9 1.3 %copy.60 = f32[256,1024]{1,0:T(8,128)} copy(f32[256,1024]{0,1:T(8,128)S(1)} %bitcast.72) | data formatting | bytes 2097152 | tf_op jit(solution)/shard_map/reshape | solution.py:75
  (36 shorter events, 1.1 us)
Async XLA Ops:
  0.0 1.4 %copy-start = (bf16[256,1024]{1,0:T(8,128)(2,1)S(1)}, bf16[256,1024]{1,0:T(8,128)(2,1)}, u32[]{:S(2)}) copy-start(bf16[256,1024]{1,0:T(8,128)(2,1)} %param.7) | copy-start | bytes 1572868
  0.0 12.3 %copy-start.1 = (s32[2,32,11]{1,0,2:T(2,128)S(1)}, s32[2,32,11]{1,0,2:T(2,128)}, u32[]{:S(2)}) copy-start(s32[2,32,11]{1,0,2:T(2,128)} %param.12) | copy-start | bytes 8452
  0.0 14.1 %copy-start.2 = (s32[2,16]{1,0:T(2,128)S(1)}, s32[2,16]{1,0:T(2,128)}, u32[]{:S(2)}) copy-start(s32[2,16]{1,0:T(2,128)} %param.10) | copy-start | bytes 388
  3.5 55.5 %all-to-all-start = ((bf16[8,1,128,1024]{3,2,1,0:T(8,128)(2,1)}), bf16[8,1,128,1024]{3,2,1,0:T(8,128)(2,1)S(1)}, u32[]{:S(2)}, u32[]{:S(2)}) async-start(bf16[8,1,128,1024]{3,2,1,0:T(8,128)(2,1)} %bitcast.68), calls=%async_computation | async-start | bytes 4194304 | tf_op jit(solution)/shard_map/all_to_all | solution.py:55
  73.8 6.7 %copy-start.3 = (s32[2,32]{1,0:T(2,128)S(1)}, s32[2,32]{1,0:T(2,128)}, u32[]{:S(2)}) copy-start(s32[2,32]{1,0:T(2,128)} %param.13) | copy-start | bytes 772
  73.8 18.1 %all-to-all-start.1 = ((bf16[2,256,4,2,128]{4,1,0,3,2:T(8,128)(2,1)}), bf16[2,256,4,2,128]{4,1,0,3,2:T(8,128)(2,1)S(1)}, u32[]{:S(2)}, u32[]{:S(2)}) async-start(bf16[2,256,4,2,128]{4,1,0,3,2:T(8,128)(2,1)} %bitcast.15), calls=%async_computation.1 | async-start | bytes 2097152 | tf_op jit(solution)/shard_map/all_to_all | solution.py:62
where the time goes:
time: 113 us
  waiting for transfers between devices  55.9 us (49%)
  local copies, waits for them, and re-layouts  28.1 us (25%)
  matrix products  16.4 us (15%)
  starting transfers between devices  10.9 us (10%)
  other arithmetic  1.75 us (2%)
    all_to_all x1, waiting for transfers between devices, on_device(): lax.all_to_all(outgoing, 'alpha', split_axis=0, concat_axis=0, tiled=True)  44.7 us
    all_to_all x1, waiting for transfers between devices, on_device(): lax.all_to_all(outgoing_cols, 'beta', split_axis=2, concat_axis=2, tiled=...  11.2 us
    gather x2, local copies, waits for them, and re-layouts, pick_columns(): return pool_piece[:, index_piece]  10.2 us
    dot_general x1, matrix products, on_device(): jnp.einsum('kabsj,kbrsj->abr', picked, beta_kept, preferred_element_type=...  9.82 us
    all_to_all x1, starting transfers between devices, on_device(): lax.all_to_all(outgoing, 'alpha', split_axis=0, concat_axis=0, tiled=True)  7.29 us
    dot_general x1, matrix products, on_device(): jnp.einsum('kbrsi,kbsic->kbrc', alpha_kept, chosen, preferred_element_typ...  6.58 us
    gather x1, local copies, waits for them, and re-layouts, on_device(): incoming.reshape(alpha_size * row_capacity, block_size, local_cols)  6.09 us
    gather x4, local copies, waits for them, and re-layouts, locate(): return owner * capacity + ranking_here[owner, local_id] - 1  3.96 us
  transfers between devices with their start and end apart: 2, of which 2 were waited for; matrix products, arithmetic and copies ran while one was open for 6% of the time, Pallas kernels for 0%

commit v1 on v0

--- a/solution.py
+++ b/solution.py
@@ -1,10 +1,363 @@
+import functools
+
 import jax
 import jax.numpy as jnp
 from jax import lax
+from jax.experimental import pallas as pl
+from jax.experimental.pallas import tpu as pltpu
 from jax.sharding import PartitionSpec as P
 
 FROM_A = 1
 FROM_B = 2
+PAIR = 2
+VMEM_LIMIT = 60 * 1024 * 1024
+MESH = pl.DeviceIdType.MESH
+
+
+def pick_kernel(geometry, a_lists, b_lists, c_ref, picks_ref, small):
+    na, nb, ops, slots, blk, row_blocks, col_blocks = geometry
+    a = lax.axis_index("alpha")
+    c = lax.axis_index("beta")
+    lists = b_lists[...]
+    lane = lax.broadcasted_iota(jnp.int32, (1, nb * col_blocks), 1)
+
+    def extremes(receiver, owner):
+        local = lists - owner * col_blocks
+        hit = (local >= 0) & (local < col_blocks)
+        rows_here = (lane >= receiver * col_blocks) & (lane < (receiver + 1) * col_blocks)
+        low = jnp.min(jnp.min(jnp.where(hit, local, col_blocks), axis=0), axis=0, keepdims=True)
+        high = jnp.max(jnp.max(jnp.where(hit, local, 0), axis=0), axis=0, keepdims=True)
+        low = jnp.min(jnp.where(rows_here, low, col_blocks))
+        high = jnp.max(jnp.where(rows_here, high, 0))
+        return jnp.where(low < col_blocks, low, 0), high
+
+    for j in range(nb):
+        for u, block in enumerate(extremes(c ^ j, c)):
+            picks_ref[j, :, u * blk:(u + 1) * blk] = c_ref[:, pl.ds(pl.multiple_of(block * blk, blk), blk)]
+    for owner in range(nb):
+        small[2 * na + owner] = extremes(c, owner)[0]
+    for n in range(2 * na):
+        small[n] = 0
+    for side in range(2):
+        receiver = a ^ side
+        for k in range(ops):
+            for i in range(row_blocks):
+                for s in range(slots):
+                    entry = a_lists[s, k, receiver * row_blocks + i]
+                    owner = lax.div(entry, row_blocks)
+                    small[side * na + owner] = entry - owner * row_blocks
+
+
+def sigma_kernel(geometry, small, a_lists, a_counts, b_lists, b_counts, picks, a_hbm, b_hbm, out_ref, abuf, bbuf, column, across, chosen, adense, bdense, acc,
+                 local_sem, beta_send, beta_recv, column_recv, up_send, down_send, across_send, across_recv):
+    na, nb, ops, slots, blk, row_blocks, col_blocks = geometry
+    levels = na // PAIR
+    rows = row_blocks * blk
+    wide = FROM_B * blk
+    a = lax.axis_index("alpha")
+    c = lax.axis_index("beta")
+    z = a // PAIR
+    x = a % PAIR
+    partner = a + 1 - 2 * x
+    at_low = 2 * na
+
+    def one_hot(value, place):
+        gap = value - place
+        return (1 - jnp.minimum(jnp.maximum(gap, -gap), 1)).astype(jnp.float32)
+
+    def at_most(slot, count):
+        return jnp.minimum(jnp.maximum(count - slot, 0), 1)
+
+    copy_a = pltpu.make_async_copy(a_hbm, abuf, local_sem.at[0])
+    copy_b = pltpu.make_async_copy(b_hbm, bbuf, local_sem.at[1])
+    copy_a.start()
+    copy_b.start()
+
+    column[z, 0] = picks[0]
+
+    barrier = pltpu.get_barrier_semaphore()
+    for j in range(1, nb):
+        pl.semaphore_signal(barrier, inc=1, device_id={"beta": c ^ j}, device_id_type=MESH)
+    pl.semaphore_signal(barrier, inc=1, device_id={"alpha": partner}, device_id_type=MESH)
+
+    @pl.when(z < levels - 1)
+    def _():
+        pl.semaphore_signal(barrier, inc=1, device_id={"alpha": a + PAIR}, device_id_type=MESH)
+
+    @pl.when(z > 0)
+    def _():
+        pl.semaphore_signal(barrier, inc=1, device_id={"alpha": a - PAIR}, device_id_type=MESH)
+
+    neighbours = nb + jnp.where(z < levels - 1, 1, 0) + jnp.where(z > 0, 1, 0)
+    pl.semaphore_wait(barrier, neighbours)
+
+    def beta_copy(j):
+        return pltpu.make_async_remote_copy(
+            src_ref=picks.at[j], dst_ref=column.at[z, j], send_sem=beta_send.at[j - 1], recv_sem=beta_recv.at[j - 1],
+            device_id={"beta": c ^ j}, device_id_type=MESH)
+
+    def up_copy(lev, j):
+        return pltpu.make_async_remote_copy(
+            src_ref=column.at[lev, j], dst_ref=column.at[lev, j], send_sem=up_send.at[lev, j], recv_sem=column_recv.at[lev, j],
+            device_id={"alpha": a + PAIR}, device_id_type=MESH)
+
+    def down_copy(lev, j):
+        return pltpu.make_async_remote_copy(
+            src_ref=column.at[lev, j], dst_ref=column.at[lev, j], send_sem=down_send.at[lev, j], recv_sem=column_recv.at[lev, j],
+            device_id={"alpha": a - PAIR}, device_id_type=MESH)
+
+    def across_copy(lev, j):
+        return pltpu.make_async_remote_copy(
+            src_ref=chosen.at[lev, j], dst_ref=across.at[lev, j], send_sem=across_send.at[lev, j], recv_sem=across_recv.at[lev, j],
+            device_id={"alpha": partner}, device_id_type=MESH)
+
+    for j in range(1, nb):
+        beta_copy(j).start()
+
+    acc[...] = jnp.zeros_like(acc)
+    out_ref[...] = jnp.zeros_like(out_ref)
+
+    def build_a():
+        copy_a.wait()
+
+        def per_owner(o, carry):
+            for k in range(ops):
+                for i in range(row_blocks):
+                    total = jnp.zeros((blk, blk), jnp.float32)
+                    for s in range(slots):
+                        entry = a_lists[s, k, a * row_blocks + i]
+                        valid = at_most(s, a_counts[k, a * row_blocks + i])
+                        weight = one_hot(lax.div(entry, row_blocks), o) * valid.astype(jnp.float32)
+                        total += abuf[k, s, i * blk:(i + 1) * blk, :].astype(jnp.float32) * weight
+                    high = total.astype(jnp.bfloat16)
+                    low = (total - high.astype(jnp.float32)).astype(jnp.bfloat16)
+                    at = k * rows + i * blk
+                    adense[o, 0, at:at + blk, :] = high
+                    adense[o, 1, at:at + blk, :] = low
+            return carry
+
+        lax.fori_loop(0, na, per_owner, 0)
+
+    def build_b(piece):
+        k = piece // col_blocks
+        r = piece % col_blocks
+        here = pl.ds(pl.multiple_of(r * blk, blk), blk)
+        codes = []
+        for s in range(slots):
+            entry = b_lists[s, k, c * col_blocks + r]
+            owner = lax.div(entry, col_blocks)
+            gap = entry - owner * col_blocks - small[at_low + owner]
+            place = (owner ^ c) * FROM_B + jnp.minimum(jnp.maximum(gap, -gap), 1)
+            valid = at_most(s, b_counts[k, c * col_blocks + r])
+            codes.append((place + 1) * valid - 1)
+
+        def per_chunk(j, carry):
+            for u in range(FROM_B):
+                total = jnp.zeros((blk, blk), jnp.float32)
+                for s in range(slots):
+                    weight = one_hot(codes[s], j * FROM_B + u)
+                    total += bbuf[k, s, here, :].astype(jnp.float32) * weight
+                high = total.astype(jnp.bfloat16)
+                low = (total - high.astype(jnp.float32)).astype(jnp.bfloat16)
+                bdense[j, 0, k, here, u * blk:(u + 1) * blk] = high
+                bdense[j, 1, k, here, u * blk:(u + 1) * blk] = low
+            return carry
+
+        lax.fori_loop(0, nb, per_chunk, 0)
+
+    pieces = ops * col_blocks
+
+    def selected(lev, j, pick):
+        total = jnp.zeros((blk, wide), jnp.float32)
+        for i in range(row_blocks):
+            total += column[lev, j, i * blk:(i + 1) * blk, :].astype(jnp.float32) * one_hot(pick, i)
+        return total.astype(jnp.bfloat16)
+
+    wave = 2 * levels
+    waves = levels + nb - 1
+
+    def place_of(n):
+        distance = (n // 2) % levels
+        upper = n % 2
+        j = n // wave - distance
+        lev = z + distance * (2 * upper - 1)
+        valid = (j >= 0) & (j < nb) & (lev >= 0) & (lev < levels) & (distance + 1 > upper)
+        return lev, j, distance, valid
+
+    def accumulate(owner, j, value):
+        acc[j] += (jnp.dot(adense[owner, 0], value, preferred_element_type=jnp.float32)
+                   + jnp.dot(adense[owner, 1], value, preferred_element_type=jnp.float32))
+
+    def along(m):
+        lev, j, distance, valid = place_of(m)
+
+        @pl.when(valid)
+        def _():
+            @pl.when((distance == 0) & (j > 0))
+            def _():
+                pltpu.make_async_remote_copy(
+                    src_ref=picks.at[1], dst_ref=column.at[z, j], send_sem=beta_send.at[0], recv_sem=beta_recv.at[jnp.maximum(j, 1) - 1],
+                    device_id={"beta": c ^ 1}, device_id_type=MESH).wait_recv()
+
+            @pl.when(distance > 0)
+            def _():
+                across_like = pltpu.make_async_remote_copy(
+                    src_ref=column.at[lev, j], dst_ref=column.at[lev, j], send_sem=up_send.at[lev, j], recv_sem=column_recv.at[lev, j],
+                    device_id={"alpha": partner}, device_id_type=MESH)
+                across_like.wait_recv()
+
+            @pl.when((lev <= z) & (z < levels - 1))
+            def _():
+                up_copy(lev, j).start()
+
+            @pl.when((lev >= z) & (z > 0))
+            def _():
+                down_copy(lev, j).start()
+
+            owner = lev * PAIR + x
+            chosen[lev, j] = selected(lev, j, small[na + owner])
+
+            @pl.when(m == 0)
+            def _():
+                build_a()
+
+            accumulate(owner, j, selected(lev, j, small[owner]))
+            across_copy(lev, j).start()
+
+    def over(m):
+        lev, j, distance, valid = place_of(m)
+
+        @pl.when(valid)
+        def _():
+            across_copy(lev, j).wait_recv()
+            accumulate(lev * PAIR + 1 - x, j, across[lev, j])
+
+    steps = waves * wave
+    tile = min(2, col_blocks) * blk
+
+    def finish(j):
+        inters = [acc[j, k * rows:(k + 1) * rows, :].astype(jnp.bfloat16) for k in range(ops)]
+
+        def columns(n, carry):
+            here = pl.ds(pl.multiple_of(n * tile, tile), tile)
+            total = out_ref[:, here]
+            for k in range(ops):
+                for half in range(2):
+                    total += lax.dot_general(inters[k], bdense[j, half, k, here, :], (((1,), (1,)), ((), ())),
+                                             preferred_element_type=jnp.float32)
+            out_ref[:, here] = total
+            return carry
+
+        lax.fori_loop(0, col_blocks * blk // tile, columns, 0)
+
+    def step(m, carry):
+        @pl.when(m < steps)
+        def _():
+            along(m)
+
+        piece = m - wave
+
+        @pl.when(piece == 0)
+        def _():
+            copy_b.wait()
+
+        @pl.when((piece >= 0) & (piece < pieces))
+        def _():
+            build_b(piece)
+
+        @pl.when(m >= wave)
+        def _():
+            over(m - wave)
+
+        done = m // wave - levels
+
+        @pl.when((m % wave == wave - 1) & (done >= 0))
+        def _():
+            finish(done)
+
+        return carry
+
+    lax.fori_loop(0, steps + wave, step, 0)
+
+    for j in range(1, nb):
+        beta_copy(j).wait_send()
+
+    def drain(n, carry):
+        lev = n // nb
+        j = n % nb
+
+        @pl.when((lev <= z) & (z < levels - 1))
+        def _():
+            up_copy(lev, j).wait_send()
+
+        @pl.when((lev >= z) & (z > 0))
+        def _():
+            down_copy(lev, j).wait_send()
+
+        across_copy(lev, j).wait_send()
+        return carry
+
+    lax.fori_loop(0, levels * nb, drain, 0)
+
+
+def scratch_of(geometry, dtype):
+    na, nb, ops, slots, blk, row_blocks, col_blocks = geometry
+    levels = na // PAIR
+    rows, cols, wide = row_blocks * blk, col_blocks * blk, FROM_B * blk
+    return [
+        ((ops, slots, rows, blk), dtype),
+        ((ops, slots, cols, blk), dtype),
+        ((levels, nb, rows, wide), dtype),
+        ((levels, nb, blk, wide), dtype),
+        ((levels, nb, blk, wide), dtype),
+        ((na, 2, ops * rows, blk), dtype),
+        ((nb, 2, ops, cols, wide), dtype),
+        ((nb, ops * rows, wide), jnp.float32),
+    ]
+
+
+def scratch_bytes(geometry):
+    total = 0
+    for shape, dtype in scratch_of(geometry, jnp.bfloat16):
+        size = jnp.dtype(dtype).itemsize
+        for extent in shape:
+            size *= extent
+        total += size
+    return total
+
+
+def fused(geometry, coeffs, a_blocks, a_list, a_count, b_blocks, b_list, b_count):
+    na, nb, ops, slots, blk, row_blocks, col_blocks = geometry
+    levels = na // PAIR
+    a_lists = jnp.transpose(a_list, (2, 0, 1))
+    b_lists = jnp.transpose(b_list, (2, 0, 1))
+    rows, cols = row_blocks * blk, col_blocks * blk
+    dma = pltpu.SemaphoreType.DMA
+    smem = pl.BlockSpec(memory_space=pltpu.SMEM)
+    vmem = pl.BlockSpec(memory_space=pltpu.VMEM)
+    picks, small = pl.pallas_call(
+        functools.partial(pick_kernel, geometry),
+        out_shape=(jax.ShapeDtypeStruct((nb, rows, FROM_B * blk), coeffs.dtype), jax.ShapeDtypeStruct((2 * na + nb,), jnp.int32)),
+        in_specs=[smem, vmem, vmem],
+        out_specs=(vmem, smem),
+        name="pick_blocks",
+    )(a_lists, b_lists, coeffs)
+    return pl.pallas_call(
+        functools.partial(sigma_kernel, geometry),
+        out_shape=jax.ShapeDtypeStruct((rows, cols), jnp.float32),
+        in_specs=[
+            smem, smem, smem, smem, smem, vmem,
+            pl.BlockSpec(memory_space=pl.ANY),
+            pl.BlockSpec(memory_space=pl.ANY),
+        ],
+        out_specs=pl.BlockSpec(memory_space=pltpu.VMEM),
+        scratch_shapes=[pltpu.VMEM(shape, dtype) for shape, dtype in scratch_of(geometry, coeffs.dtype)] + [
+            dma((2,)), dma((nb - 1,)), dma((nb - 1,)), dma((levels, nb)), dma((levels, nb)), dma((levels, nb)),
+            dma((levels, nb)), dma((levels, nb)),
+        ],
+        compiler_params=pltpu.CompilerParams(collective_id=0, has_side_effects=True, vmem_limit_bytes=VMEM_LIMIT),
+        name="sigma_build",
+    )(small, a_lists, a_count, b_lists, b_count, picks, jnp.transpose(a_blocks, (0, 2, 1, 3)), jnp.transpose(b_blocks, (0, 2, 1, 3)))
 
 
 def arrange(entries, owners, per_owner, capacity):
@@ -30,7 +383,7 @@
     return pool_piece[:, index_piece]
 
 
-def on_device(coeffs, a_blocks, a_list, a_count, b_blocks, b_list, b_count):
+def plain(coeffs, a_blocks, a_list, a_count, b_blocks, b_list, b_count):
     operators, local_rows, list_slots, block_size = a_blocks.shape
     local_cols = coeffs.shape[1]
     row_blocks = local_rows // block_size
@@ -75,6 +428,16 @@
     return sigma.reshape(local_rows, local_cols)
 
 
+def on_device(coeffs, a_blocks, a_list, a_count, b_blocks, b_list, b_count):
+    operators, local_rows, list_slots, block_size = a_blocks.shape
+    na, nb = lax.axis_size("alpha"), lax.axis_size("beta")
+    geometry = (na, nb, operators, list_slots, block_size, local_rows // block_size, coeffs.shape[1] // block_size)
+    fits = scratch_bytes(geometry) < VMEM_LIMIT * 3 // 4
+    shaped = FROM_A == 1 and FROM_B == 2 and na % PAIR == 0 and nb & (nb - 1) == 0 and nb > 1
+    build = functools.partial(fused, geometry) if fits and shaped else plain
+    return build(coeffs, a_blocks, a_list, a_count, b_blocks, b_list, b_count)
+
+
 def solution(mesh):
     in_specs = (
         P("alpha", "beta"),

time: 113 us -> 59.4 us (0.53)
  Pallas kernels: 0 us -> 56.8 us
  waiting for transfers between devices: 55.9 us -> 0 us
  local copies, waits for them, and re-layouts: 28.1 us -> 2.31 us
  matrix products: 16.4 us -> 0 us
  starting transfers between devices: 10.9 us -> 0 us
  other arithmetic: 1.75 us -> 0 us
    pallas_call x0 -> x2, Pallas kernels: none -> 56.8 us  [the longest x1 54.5 us: fused(): pl.pallas_call(functools.partial(sigma_kernel, geometry), out_shape=jax.S...]
    all_to_all x2 -> x0, waiting for transfers between devices: 55.9 us -> none  [the longest x1 44.7 us: on_device(): lax.all_to_all(outgoing, 'alpha', split_axis=0, concat_axis=0, tiled=True)]
    gather x9 -> x0, local copies, waits for them, and re-layouts: 23.9 us -> none  [the longest x2 10.2 us: pick_columns(): return pool_piece[:, index_piece]]
    dot_general x2 -> x0, matrix products: 16.4 us -> none  [the longest x1 9.82 us: on_device(): jnp.einsum('kabsj,kbrsj->abr', picked, beta_kept, preferred_element_type=...]
    all_to_all x2 -> x0, starting transfers between devices: 10.9 us -> none  [the longest x1 7.29 us: on_device(): lax.all_to_all(outgoing, 'alpha', split_axis=0, concat_axis=0, tiled=True)]
    reshape x2 -> x0, local copies, waits for them, and re-layouts: 1.5 us -> none  [the longest x1 1.31 us: on_device(): return sigma.reshape(local_rows, local_cols)]
    unnamed x11 -> x1, local copies, waits for them, and re-layouts: 1.21 us -> 2.31 us
  transfers between devices with their start and end apart: 2 -> 0, of which waited for: 2 -> 0; matrix products, arithmetic and copies ran while one was open for 6% -> 0% of each run, Pallas kernels for 0% -> 0%
where the time goes in v1:
time: 59.4 us; the launch traced here: 59.2 us
  Pallas kernels  56.8 us (96%)
  local copies, waits for them, and re-layouts  2.31 us (4%)
    pallas_call x1, Pallas kernels, fused(): pl.pallas_call(functools.partial(sigma_kernel, geometry), out_shape=jax.S...  54.5 us
    pallas_call x1, Pallas kernels, fused(): pl.pallas_call(functools.partial(pick_kernel, geometry), out_shape=(jax.S...  2.36 us
    unnamed x1, local copies, waits for them, and re-layouts  2.31 us

profile of v1, /device:TPU:0, one launch (start us, length us, event | category | flops | bytes accessed | tf_op | source)
XLA Modules:
  0.0 59.2 jit_solution(3137779123849437689)
XLA Ops:
  0.0 2.4 %pick_blocks.1 = (bf16[4,256,256]{2,1,0:T(8,128)(2,1)}, s32[20]{0:T(128)}) custom-call(s32[11,2,16]{2,1,0:T(2,128)} %bitcast.6, s32[11,2,32]{2,1,0:T(2,128)} %bitcast.8, bf16[256,1024]{1,0:T(8,128)(2,1)} %c_ref.1), custom_call_target="tpu_custom_call" | custom-call | tf_op jit(solution)/shard_map/pick_blocks/pallas_call | solution.py:338
  2.4 54.5 %sigma_build.1 = f32[256,1024]{1,0:T(8,128)} custom-call(s32[20]{0:T(128)} %get-tuple-element.7.small, s32[11,2,16]{2,1,0:T(2,128)} %bitcast.7, s32[2,16]{1,0:T(2,128)} %a_counts.1, s32[11,2,32]{2,1,0:T(2,128)} %bitcast.9, s32[2,32]{1,0:T(2,128)} %b_counts.1, bf16[4,256,256]{2,1,0:T(8,128)(2,1)} %get-tuple-element.8.picks, ...), custom_call_target="tpu_custom_call" | custom-call | tf_op jit(solution)/shard_map/sigma_build/pallas_call | solution.py:345
  56.9 2.3 %copy.9 = f32[256,1024]{1,0:T(8,128)} copy(f32[256,1024]{1,0:T(8,128)} %sigma_build.1) | data formatting | bytes 2097152

commit v2 on v1

--- a/solution.py
+++ b/solution.py
@@ -206,6 +206,9 @@
                     device_id={"alpha": partner}, device_id_type=MESH)
                 across_like.wait_recv()
 
+            owner = lev * PAIR + x
+            chosen[lev, j] = selected(lev, j, small[na + owner])
+
             @pl.when((lev <= z) & (z < levels - 1))
             def _():
                 up_copy(lev, j).start()
@@ -214,15 +217,13 @@
             def _():
                 down_copy(lev, j).start()
 
-            owner = lev * PAIR + x
-            chosen[lev, j] = selected(lev, j, small[na + owner])
+            across_copy(lev, j).start()
 
             @pl.when(m == 0)
             def _():
                 build_a()
 
             accumulate(owner, j, selected(lev, j, small[owner]))
-            across_copy(lev, j).start()
 
     def over(m):
         lev, j, distance, valid = place_of(m)

time: 59.4 us -> 57.6 us (0.970)
  Pallas kernels: 56.8 us -> 55 us
    pallas_call x1, Pallas kernels: 54.5 us -> 52.7 us  [fused(): pl.pallas_call(functools.partial(sigma_kernel, geometry), out_shape=jax.S...]
where the time goes in v2:
time: 57.6 us; the launch traced here: 57.3 us
  Pallas kernels  55 us (95%)
  local copies, waits for them, and re-layouts  2.31 us (4%)
    pallas_call x1, Pallas kernels, fused(): pl.pallas_call(functools.partial(sigma_kernel, geometry), out_shape=jax.S...  52.7 us
    pallas_call x1, Pallas kernels, fused(): pl.pallas_call(functools.partial(pick_kernel, geometry), out_shape=(jax.S...  2.36 us
    unnamed x1, local copies, waits for them, and re-layouts  2.31 us

profile of v2, /device:TPU:0, one launch (start us, length us, event | category | flops | bytes accessed | tf_op | source)
XLA Modules:
  0.0 57.3 jit_solution(1372538321498061575)
XLA Ops:
  0.0 2.4 %pick_blocks.1 = (bf16[4,256,256]{2,1,0:T(8,128)(2,1)}, s32[20]{0:T(128)}) custom-call(s32[11,2,16]{2,1,0:T(2,128)} %bitcast.6, s32[11,2,32]{2,1,0:T(2,128)} %bitcast.8, bf16[256,1024]{1,0:T(8,128)(2,1)} %c_ref.1), custom_call_target="tpu_custom_call" | custom-call | tf_op jit(solution)/shard_map/pick_blocks/pallas_call | solution.py:339
  2.4 52.7 %sigma_build.1 = f32[256,1024]{1,0:T(8,128)} custom-call(s32[20]{0:T(128)} %get-tuple-element.7.small, s32[11,2,16]{2,1,0:T(2,128)} %bitcast.7, s32[2,16]{1,0:T(2,128)} %a_counts.1, s32[11,2,32]{2,1,0:T(2,128)} %bitcast.9, s32[2,32]{1,0:T(2,128)} %b_counts.1, bf16[4,256,256]{2,1,0:T(8,128)(2,1)} %get-tuple-element.8.picks, ...), custom_call_target="tpu_custom_call" | custom-call | tf_op jit(solution)/shard_map/sigma_build/pallas_call | solution.py:346
  55.0 2.3 %copy.9 = f32[256,1024]{1,0:T(8,128)} copy(f32[256,1024]{1,0:T(8,128)} %sigma_build.1) | data formatting | bytes 2097152
